TPU v7x, 128 devices: a whole 4x4x4 slice. The times are simulated.
128 devices in a mesh: row: 16 (over x, y), col: 8 (over z, core).
Axes of the slice: x: 4, y: 4, z: 4, core: 2. Of those that a mesh axis runs over, the one named last changes fastest.
Arguments:
- rhs_rows: float32 [65536, 256], P(('row', 'col')), may hold values from -6 to 6
- dest_row: int32 [65536], P(('row', 'col')), may hold values from 0 to 65535, as said below
- diag_inverse: bfloat16 [4, 128, 128, 128], P(None, ('row', 'col')), may hold values from -1 to 1.5, as said below
- lower_blocks: bfloat16 [3, 16, 8, 128, 8, 16, 128], P(None, 'row', None, None, 'col'), may hold values from -0.046875 to 0.046875
- block_mask: int32 [3, 16, 8, 8, 16], P(None, 'row', None, 'col'), may hold values 0 or 1
Outputs:
- solution: bfloat16 [4, 128, 128, 256], P(None, ('row', 'col'))
Inputs may be any that keep to these rules, and one draw needn't show every extreme that they name: dest_row is a permutation of the rows. In each aligned block of 512 entries, exactly 4 entries g have (g // 128) % 128 equal to q, for every supernode index q. `diag_inverse`: every block is lower triangular with positive diagonal entries.
All inputs are finite; a program needn't handle non-finite values. No bound on the sum of `block_mask` on one device may be relied on, other than what follows from the above.
Results may differ from a plain program's by a relative error of at most 0.029.
Values may be sent and summed in bfloat16 or wider, within the bound.
A program may use at most 128 MiB of HBM per device.

v0:
```python
import jax
import jax.numpy as jnp
from jax import lax
from jax.sharding import PartitionSpec as P

B = 128
NLEV = 4


def per_device(rhs_rows, dest_row, diag_inverse, lower_blocks, block_mask):
    col_count = lax.axis_size("col")
    row_count = lax.axis_size("row")
    supernodes = row_count * col_count
    local_rows = rhs_rows.shape[0]
    column_total = rhs_rows.shape[1]
    group_rows = local_rows // supernodes
    owner_idx = dest_row // B % supernodes
    position = dest_row // (supernodes * B) * B + dest_row % B
    sort_order = jnp.argsort(owner_idx, stable=True)
    sending = rhs_rows[sort_order]
    places = position[sort_order]
    arrived, arrived_pos = (
        lax.all_to_all(
            sending.reshape(supernodes, group_rows, column_total).astype(jnp.bfloat16),
            ("row", "col"),
            split_axis=0,
            concat_axis=0,
            tiled=True,
        ).astype(jnp.float32),
        lax.all_to_all(
            places.reshape(supernodes, group_rows),
            ("row", "col"),
            split_axis=0,
            concat_axis=0,
            tiled=True,
        ),
    )
    ordered = (
        jnp.zeros_like(rhs_rows)
        .at[arrived_pos.reshape(local_rows)]
        .set(arrived.reshape(local_rows, column_total))
    )
    ordered = ordered.reshape(NLEV, B, column_total)
    diag_inv = diag_inverse[:, 0]
    masked = []
    for level_idx in range(NLEV - 1):
        block_tile = lower_blocks[level_idx, 0, :, :, 0]
        tile_mask = block_mask[level_idx, 0, :, 0, :].astype(jnp.bfloat16)
        masked.append(
            (block_tile * tile_mask[:, None, :, None]).reshape(col_count * B, row_count * B)
        )
    column_count = ordered.shape[2]
    solved = []
    for level_idx in range(NLEV):
        if level_idx == 0:
            residual = ordered[0].astype(jnp.bfloat16)
        else:
            level_tile = masked[level_idx - 1]

            def add_piece(running, shard_piece, first_row, level_tile=level_tile):
                return jnp.dot(level_tile, shard_piece, preferred_element_type=jnp.float32)

            start_sum = jnp.zeros((col_count * B, column_count), jnp.float32)
            partial_sum = add_piece(
                start_sum,
                lax.all_gather(solved[level_idx - 1], "row", axis=0, tiled=True),
                jnp.int32(0),
            )
            coupled = lax.psum_scatter(
                partial_sum.astype(jnp.bfloat16), "col", scatter_dimension=0, tiled=True
            ).astype(jnp.float32)
            residual = (ordered[level_idx] - coupled).astype(jnp.bfloat16)
        solved.append(
            jnp.dot(diag_inv[level_idx], residual, preferred_element_type=jnp.float32).astype(
                jnp.bfloat16
            )
        )
    solution = [None] * NLEV
    for level_idx in range(NLEV - 1, -1, -1):
        if level_idx == NLEV - 1:
            residual = solved[level_idx]
        else:
            upper_blocks = lax.all_gather(solution[level_idx + 1], "col", axis=0, tiled=True)
            level_tile = masked[level_idx]

            def column_term(first_row, row_span, level_tile=level_tile, upper_blocks=upper_blocks):
                return lax.dot_general(
                    level_tile,
                    upper_blocks,
                    (((0,), (0,)), ((), ())),
                    preferred_element_type=jnp.float32,
                )

            back_coupled = lax.psum_scatter(
                column_term(jnp.int32(0), B * lax.axis_size("row")).astype(jnp.bfloat16),
                "row",
                scatter_dimension=0,
                tiled=True,
            ).astype(jnp.float32)
            residual = (solved[level_idx].astype(jnp.float32) - back_coupled).astype(jnp.bfloat16)
        product = lax.dot_general(
            diag_inv[level_idx],
            residual,
            (((0,), (0,)), ((), ())),
            preferred_element_type=jnp.float32,
        )
        solution[level_idx] = product.astype(jnp.bfloat16)
    results = jnp.stack(solution)
    return results[:, None]


def solution(mesh):
    in_specs = (
        P(("row", "col"), None),
        P(("row", "col")),
        P(None, ("row", "col"), None, None),
        P(None, "row", None, None, "col", None, None),
        P(None, "row", None, "col", None),
    )
    out_specs = P(None, ("row", "col"), None, None)
    return jax.shard_map(
        per_device, mesh=mesh, in_specs=in_specs, out_specs=out_specs, check_vma=False
    )
```

profile of v0, /device:TPU:0, one launch (start us, length us, event | category | flops | bytes accessed | tf_op | source)
XLA Modules:
  0.0 586.9 jit_solution(4313193197530527790)
XLA Ops:
  6.5 0.8 add_select_fusion
  7.3 3.8 sort.17
  11.1 3.5 gather_fusion
  14.6 0.7 all_to_all.9
  15.3 11.1 %all-to-all-start = ((s32[128,1,4]{2,1,0:T(1,128)}), s32[128,1,4]{2,1,0:T(1,128)S(1)}, u32[]{:S(2)}, u32[]{:S(2)}) async-start(s32[128,1,4]{2,1,0:T(1,128)} %bitcast), calls=%async_computation | async-start | bytes 131072 | tf_op jit(solution)/shard_map/all_to_all | solution.py:30
  26.5 1.6 gather_fusion.1
  28.0 0.8 convert_element_type.143
  28.8 7.2 %all-to-all-done = s32[128,1,4]{2,1,0:T(1,128)S(1)} async-done(((s32[128,1,4]{2,1,0:T(1,128)}), s32[128,1,4]{2,1,0:T(1,128)S(1)}, u32[]{:S(2)}, u32[]{:S(2)}) %all-to-all-start) | async-done | bytes 2080 | tf_op jit(solution)/shard_map/all_to_all | solution.py:30
  36.0 4.6 all-to-all-start.1
  41.2 0.8 reduce.3
  42.1 9.4 %all-to-all-done.1 = bf16[128,4,256]{2,1,0:T(4,128)(2,1)S(1)} async-done(((bf16[128,4,256]{2,1,0:T(4,128)(2,1)}), bf16[128,4,256]{2,1,0:T(4,128)(2,1)S(1)}, u32[]{:S(2)}, u32[]{:S(2)}) %all-to-all-start.1) | async-done | bytes 262176 | tf_op jit(solution)/shard_map/all_to_all | solution.py:23
  51.6 2.4 scatter_custom_fusion
  54.0 0.8 fusion
  54.9 8.8 %fusion.34 = (bf16[1,1,8,128,1,16,128]{6,5,4,3,2,1,0:T(8,128)(2,1)}, bf16[1,1,8,128,1,16,128]{6,5,4,3,2,1,0:T(8,128)(2,1)}, bf16[1,1,8,128,1,16,128]{6,5,4,3,2,1,0:T(8,128)(2,1)}) fusion(bf16[3,1,8,128,1,16,128]{6,5,4,3,2,1,0:T(8,128)(2,1)} %param.8), kind=kLoop, calls=%fused_computation.74 | loop fusion | bytes 25165824 | tf_op jit(solution)/shard_map/slice | solution.py:47
  63.7 30.4 %all-gather.4.cloned.1.call-done = bf16[2048,256]{0,1:T(8,128)(2,1)} async-done(((bf16[128,256]{0,1:T(8,128)(2,1)}), bf16[2048,256]{0,1:T(8,128)(2,1)}) %all-gather.4.cloned.1.call-update) | async-done | bytes 1048592 | tf_op jit(solution)/shard_map/all_gather | solution.py:66
  94.1 0.6 mul.41
  94.7 2.1 copy-done.1
  96.8 1.0 copy-done.4
  97.8 3.7 convolution_convert_fusion.5
  101.6 30.6 %reduce-scatter.13.cloned.1.call-done = bf16[128,256]{1,0:T(8,128)(2,1)} async-done(((bf16[1024,256]{1,0:T(8,128)(2,1)}), bf16[128,256]{1,0:T(8,128)(2,1)}) %reduce-scatter.13.cloned.1.call-update) | async-done | bytes 65552 | tf_op jit(solution)/shard_map/reduce_scatter | solution.py:69
  132.2 1.7 fusion.1
  133.9 42.6 %all-gather.6.cloned.1.call-done = bf16[2048,256]{0,1:T(8,128)(2,1)} async-done(((bf16[128,256]{0,1:T(8,128)(2,1)}), bf16[2048,256]{0,1:T(8,128)(2,1)}) %all-gather.6.cloned.1.call-update) | async-done | bytes 1048592 | tf_op jit(solution)/shard_map/all_gather | solution.py:66
  176.5 0.6 mul.44
  177.1 2.1 copy-done.2
  179.3 1.0 copy-done.5
  180.2 3.7 convolution_convert_fusion.4
  184.0 30.6 %reduce-scatter.15.cloned.1.call-done = bf16[128,256]{1,0:T(8,128)(2,1)} async-done(((bf16[1024,256]{1,0:T(8,128)(2,1)}), bf16[128,256]{1,0:T(8,128)(2,1)}) %reduce-scatter.15.cloned.1.call-update) | async-done | bytes 65552 | tf_op jit(solution)/shard_map/reduce_scatter | solution.py:69
  214.6 1.7 fusion.2
  216.5 42.1 %all-gather.8.cloned.1.call-done = bf16[2048,256]{0,1:T(8,128)(2,1)} async-done(((bf16[128,256]{0,1:T(8,128)(2,1)}), bf16[2048,256]{0,1:T(8,128)(2,1)}) %all-gather.8.cloned.1.call-update) | async-done | bytes 1048592 | tf_op jit(solution)/shard_map/all_gather | solution.py:66
  258.6 0.6 mul.47
  259.2 2.1 copy-done.3
  261.3 1.0 copy-done.6
  262.3 3.7 convolution_convert_fusion.3
  266.0 30.6 %reduce-scatter.17.cloned.1.call-done = bf16[128,256]{1,0:T(8,128)(2,1)} async-done(((bf16[1024,256]{1,0:T(8,128)(2,1)}), bf16[128,256]{1,0:T(8,128)(2,1)}) %reduce-scatter.17.cloned.1.call-update) | async-done | bytes 65552 | tf_op jit(solution)/shard_map/reduce_scatter | solution.py:69
  296.6 1.2 convolution_convert_fusion.9
  297.8 12.2 %all_gather.21 = bf16[1024,256]{0,1:T(8,128)(2,1)S(1)} all-gather(bf16[128,256]{0,1:T(8,128)(2,1)S(1)} %bitcast.107), channel_id=1, replica_groups=mesh['row'=16,'col'=8] {'col'}, dimensions={0}, use_global_device_ids=true | all-gather | bytes 589824 | tf_op jit(solution)/shard_map/all_gather | solution.py:83
  310.0 7.7 %convolution_convert_fusion.2 = bf16[2048,256]{1,0:T(8,128)(2,1)} fusion(bf16[1024,256]{0,1:T(8,128)(2,1)S(1)} %all_gather.21, bf16[128,8,16,128]{3,2,1,0:T(8,128)(2,1)} %bitcast.100, bf16[128,8,16,128]{3,2,1,0:T(8,128)(2,1)} %bitcast.105), kind=kOutput, calls=%fused_computation.8 | convolution fusion | flops 1076363264 | bytes 9961472 | tf_op jit(solution)/shard_map/dot_general | solution.py:87
  317.8 73.9 %reduce-scatter.19.cloned.1.call-done = bf16[128,256]{1,0:T(8,128)(2,1)} async-done(((bf16[2048,256]{1,0:T(8,128)(2,1)}), bf16[128,256]{1,0:T(8,128)(2,1)}) %reduce-scatter.19.cloned.1.call-update) | async-done | bytes 65552
  391.7 0.9 copy.17
  392.8 13.3 %all_gather.22 = bf16[1024,256]{0,1:T(8,128)(2,1)S(1)} all-gather(bf16[128,256]{0,1:T(8,128)(2,1)S(1)} %bitcast.109), channel_id=1, replica_groups=mesh['row'=16,'col'=8] {'col'}, dimensions={0}, use_global_device_ids=true | all-gather | bytes 589824 | tf_op jit(solution)/shard_map/all_gather | solution.py:83
  406.1 7.6 %convolution_convert_fusion.1 = bf16[2048,256]{1,0:T(8,128)(2,1)} fusion(bf16[1024,256]{0,1:T(8,128)(2,1)S(1)} %all_gather.22, bf16[128,8,16,128]{3,2,1,0:T(8,128)(2,1)} %bitcast.98, bf16[128,8,16,128]{3,2,1,0:T(8,128)(2,1)} %bitcast.103), kind=kOutput, calls=%fused_computation.7 | convolution fusion | flops 1076363264 | bytes 9961472 | tf_op jit(solution)/shard_map/dot_general | solution.py:87
  413.8 71.0 %reduce-scatter.21.cloned.1.call-done = bf16[128,256]{1,0:T(8,128)(2,1)} async-done(((bf16[2048,256]{1,0:T(8,128)(2,1)}), bf16[128,256]{1,0:T(8,128)(2,1)}) %reduce-scatter.21.cloned.1.call-update) | async-done | bytes 65552
  484.8 0.9 copy.19
  486.0 13.6 %all_gather.23 = bf16[1024,256]{0,1:T(8,128)(2,1)S(1)} all-gather(bf16[128,256]{0,1:T(8,128)(2,1)S(1)} %bitcast.111), channel_id=1, replica_groups=mesh['row'=16,'col'=8] {'col'}, dimensions={0}, use_global_device_ids=true | all-gather | bytes 589824 | tf_op jit(solution)/shard_map/all_gather | solution.py:83
  499.5 7.7 %convolution_convert_fusion = bf16[2048,256]{1,0:T(8,128)(2,1)} fusion(bf16[1024,256]{0,1:T(8,128)(2,1)S(1)} %all_gather.23, bf16[128,8,16,128]{3,2,1,0:T(8,128)(2,1)} %bitcast.96, bf16[128,8,16,128]{3,2,1,0:T(8,128)(2,1)} %bitcast.101), kind=kOutput, calls=%fused_computation.6 | convolution fusion | flops 1076363264 | bytes 9961472 | tf_op jit(solution)/shard_map/dot_general | solution.py:87
  507.2 71.1 %reduce-scatter.23.cloned.1.call-done = bf16[128,256]{1,0:T(8,128)(2,1)} async-done(((bf16[2048,256]{1,0:T(8,128)(2,1)}), bf16[128,256]{1,0:T(8,128)(2,1)}) %reduce-scatter.23.cloned.1.call-update) | async-done | bytes 65552
  578.3 0.9 copy.21
  579.5 0.9 copy.15
  (49 shorter events, 2.0 us)
Async XLA Ops:
  6.5 19.9 %copy-start = (f32[512,256]{1,0:T(8,128)S(1)}, f32[512,256]{1,0:T(8,128)}, u32[]{:S(2)}) copy-start(f32[512,256]{1,0:T(8,128)} %param.5) | copy-start | bytes 1572868
  6.5 47.4 %copy-start.10 = (bf16[4,1,128,128]{3,2,1,0:T(8,128)(2,1)S(1)}, bf16[4,1,128,128]{3,2,1,0:T(8,128)(2,1)}, u32[]{:S(2)}) copy-start(bf16[4,1,128,128]{3,2,1,0:T(8,128)(2,1)} %param.7) | copy-start | bytes 393220
  6.5 48.3 %copy-start.11 = (s32[3,1,8,1,16]{4,3,2,1,0:T(1,128)S(1)}, s32[3,1,8,1,16]{4,3,2,1,0:T(1,128)}, u32[]{:S(2)}) copy-start(s32[3,1,8,1,16]{4,3,2,1,0:T(1,128)} %param.9) | copy-start | bytes 4612
  15.3 20.6 %all-to-all-start = ((s32[128,1,4]{2,1,0:T(1,128)}), s32[128,1,4]{2,1,0:T(1,128)S(1)}, u32[]{:S(2)}, u32[]{:S(2)}) async-start(s32[128,1,4]{2,1,0:T(1,128)} %bitcast), calls=%async_computation | async-start | bytes 131072 | tf_op jit(solution)/shard_map/all_to_all | solution.py:30
  36.0 15.6 %all-to-all-start.1 = ((bf16[128,4,256]{2,1,0:T(4,128)(2,1)}), bf16[128,4,256]{2,1,0:T(4,128)(2,1)S(1)}, u32[]{:S(2)}, u32[]{:S(2)}) async-start(bf16[128,4,256]{2,1,0:T(4,128)(2,1)} %convert_element_type.143), calls=%async_computation.1 | async-start | bytes 524288 | tf_op jit(solution)/shard_map/all_to_all | solution.py:23
  40.6 53.5 %all-gather.4.cloned.1.call-start = ((), (), s32[]{:S(2)}) async-start(), calls=%async_computation.8 | async-start | bytes 1114112 | tf_op jit(solution)/shard_map/all_gather | solution.py:66
  54.8 77.3 %reduce-scatter.13.cloned.1.call-start = ((), (), s32[]{:S(2)}) async-start(), calls=%async_computation.9 | async-start | bytes 589824 | tf_op jit(solution)/shard_map/reduce_scatter | solution.py:69
  94.1 3.7 copy-start.4
  94.7 2.1 copy-start.1
  101.5 75.0 %all-gather.6.cloned.1.call-start = ((), (), s32[]{:S(2)}) async-start(), calls=%async_computation.10 | async-start | bytes 1114112 | tf_op jit(solution)/shard_map/all_gather | solution.py:66
  133.9 80.8 %reduce-scatter.15.cloned.1.call-start = ((), (), s32[]{:S(2)}) async-start(), calls=%async_computation.11 | async-start | bytes 589824 | tf_op jit(solution)/shard_map/reduce_scatter | solution.py:69
  176.5 3.7 copy-start.5
  177.1 2.1 copy-start.2
  183.9 74.6 %all-gather.8.cloned.1.call-start = ((), (), s32[]{:S(2)}) async-start(), calls=%async_computation.12 | async-start | bytes 1114112 | tf_op jit(solution)/shard_map/all_gather | solution.py:66
  216.3 80.3 %reduce-scatter.17.cloned.1.call-start = ((), (), s32[]{:S(2)}) async-start(), calls=%async_computation.13 | async-start | bytes 589824 | tf_op jit(solution)/shard_map/reduce_scatter | solution.py:69
  258.6 3.7 copy-start.6
  259.2 2.1 copy-start.3
  266.0 125.7 %reduce-scatter.19.cloned.1.call-start = ((), (), s32[]{:S(2)}) async-start(), calls=%async_computation.14 | async-start | bytes 1114112
  310.0 82.6 %copy-start.9 = (bf16[128,256]{0,1:T(8,128)(2,1)S(1)}, bf16[128,256]{0,1:T(8,128)(2,1)}, u32[]{:S(2)}) copy-start(bf16[128,256]{0,1:T(8,128)(2,1)} %fusion.2) | copy-start | bytes 196612
  317.7 167.1 %reduce-scatter.21.cloned.1.call-start = ((), (), s32[]{:S(2)}) async-start(), calls=%async_computation.15 | async-start | bytes 1114112
  406.1 79.7 %copy-start.8 = (bf16[128,256]{0,1:T(8,128)(2,1)S(1)}, bf16[128,256]{0,1:T(8,128)(2,1)}, u32[]{:S(2)}) copy-start(bf16[128,256]{0,1:T(8,128)(2,1)} %fusion.1) | copy-start | bytes 196612
  413.8 164.6 %reduce-scatter.23.cloned.1.call-start = ((), (), s32[]{:S(2)}) async-start(), calls=%async_computation.16 | async-start | bytes 1114112
  499.5 79.8 %copy-start.7 = (bf16[128,256]{0,1:T(8,128)(2,1)S(1)}, bf16[128,256]{0,1:T(8,128)(2,1)}, u32[]{:S(2)}) copy-start(bf16[128,256]{0,1:T(8,128)(2,1)} %fusion) | copy-start | bytes 196612
Sparse Core Ops, SparseCore 0:
  55.0 39.0 all-gather.3
  101.6 30.4 reduce-scatter.12
  134.5 41.9 all-gather.5
  184.1 30.5 reduce-scatter.14
  216.6 41.9 all-gather.7
  266.1 30.4 reduce-scatter.16
  317.9 73.7 reduce-scatter.18
  413.9 70.8 reduce-scatter.20
  507.3 70.9 reduce-scatter.22
where the time goes:
time: 588 us; the launch traced here: 587 us
  waiting for transfers between devices  440 us (75%)
  matrix products  39.7 us (7%)
  blocking collectives  39.2 us (7%)
  local copies, waits for them, and re-layouts  33.2 us (6%)
  starting transfers between devices  16.3 us (3%)
  between operations  13.5 us (2%)
    unnamed x12, waiting for transfers between devices  216 us
    all_gather x3, waiting for transfers between devices, per_device(): lax.all_gather(solved[level_idx - 1], 'row', axis=0, tiled=True)  115 us
    reduce_scatter x3, waiting for transfers between devices, per_device(): lax.psum_scatter(partial_sum.astype(jnp.bfloat16), 'col', scatter_dimensi...  91.9 us
    all_gather x3, blocking collectives, per_device(): lax.all_gather(solution[level_idx + 1], 'col', axis=0, tiled=True)  39.2 us
    dot_general x3, matrix products, column_term(): lax.dot_general(level_tile, upper_blocks, (((0,), (0,)), ((), ())), prefe...  23 us
    unnamed x27, local copies, waits for them, and re-layouts  12.1 us
  transfers between devices with their start and end apart: 11, of which 11 were waited for; matrix products, arithmetic and copies ran while one was open for 2% of the time, Pallas kernels for 0%

commit v1 on v0

--- a/solution.py
+++ b/solution.py
@@ -63,7 +63,15 @@
             start_sum = jnp.zeros((col_count * B, column_count), jnp.float32)
             partial_sum = add_piece(
                 start_sum,
-                lax.all_gather(solved[level_idx - 1], "row", axis=0, tiled=True),
+                jnp.concatenate(
+                    lax.all_to_all(
+                        jnp.stack([solved[level_idx - 1]] * lax.axis_size("row"), axis=0),
+                        split_axis=0,
+                        axis_name="row",
+                        concat_axis=0,
+                    ),
+                    axis=0,
+                ),
                 jnp.int32(0),
             )
             coupled = lax.psum_scatter(

time: 588 us -> 504 us (0.86)
  waiting for transfers between devices: 440 us -> 325 us
  blocking collectives: 39.2 us -> 81.5 us
  local copies, waits for them, and re-layouts: 33.2 us -> 16.8 us
  other arithmetic: 5.37 us -> 16.9 us
  matrix products: 39.7 us -> 28.9 us
    all_gather x3 -> x0, waiting for transfers between devices: 115 us -> none  [per_device(): lax.all_gather(solved[level_idx - 1], 'row', axis=0, tiled=True)]
    all_to_all x0 -> x2, blocking collectives: none -> 41.7 us  [per_device(): lax.all_to_all(jnp.stack([solved[level_idx - 1]] * lax.axis_size('row'),...]
    slice x0 -> x1, other arithmetic: none -> 11.5 us  [per_device(): block_tile = lower_blocks[level_idx, 0, :, :, 0]]
    dot_general x3, matrix products: 23 us -> 12.3 us  [column_term(): lax.dot_general(level_tile, upper_blocks, (((0,), (0,)), ((), ())), prefe...]
    unnamed x27 -> x17, local copies, waits for them, and re-layouts: 12.1 us -> 2.87 us
    slice x1 -> x0, local copies, waits for them, and re-layouts: 8.76 us -> none  [per_device(): block_tile = lower_blocks[level_idx, 0, :, :, 0]]
    unnamed x12 -> x9, waiting for transfers between devices: 216 us -> 216 us
  transfers between devices with their start and end apart: 11 -> 9, of which waited for: 11 -> 9; matrix products, arithmetic and copies ran while one was open for 2% -> 3% of each run, Pallas kernels for 0% -> 0%
where the time goes in v1:
time: 504 us; the launch traced here: 503 us
  waiting for transfers between devices  325 us (64%)
  blocking collectives  81.5 us (16%)
  matrix products  28.9 us (6%)
  starting transfers between devices  19.7 us (4%)
  other arithmetic  16.9 us (3%)
  local copies, waits for them, and re-layouts  16.8 us (3%)
  between operations  13.8 us (3%)
    unnamed x9, waiting for transfers between devices  216 us
    reduce_scatter x3, waiting for transfers between devices, per_device(): lax.psum_scatter(partial_sum.astype(jnp.bfloat16), 'col', scatter_dimensi...  87 us
    all_to_all x2, blocking collectives, per_device(): lax.all_to_all(jnp.stack([solved[level_idx - 1]] * lax.axis_size('row'),...  41.7 us
    all_gather x3, blocking collectives, per_device(): lax.all_gather(solution[level_idx + 1], 'col', axis=0, tiled=True)  39.8 us
    dot_general x3, matrix products, add_piece(): return jnp.dot(level_tile, shard_piece, preferred_element_type=jnp.float32)  12.8 us
    dot_general x3, matrix products, column_term(): lax.dot_general(level_tile, upper_blocks, (((0,), (0,)), ((), ())), prefe...  12.3 us
    slice x1, other arithmetic, per_device(): block_tile = lower_blocks[level_idx, 0, :, :, 0]  11.5 us
    all_to_all x1, starting transfers between devices, per_device(): lax.all_to_all(places.reshape(supernodes, group_rows), ('row', 'col'), sp...  11.1 us
  transfers between devices with their start and end apart: 9, of which 9 were waited for; matrix products, arithmetic and copies ran while one was open for 3% of the time, Pallas kernels for 0%

profile of v1, /device:TPU:0, one launch (start us, length us, event | category | flops | bytes accessed | tf_op | source)
XLA Modules:
  0.0 503.0 jit_solution(7804639576022549754)
XLA Ops:
  6.5 0.8 add_select_fusion
  7.3 3.8 sort.17
  11.1 3.5 gather_fusion
  14.6 0.7 all_to_all.18
  15.3 11.1 %all-to-all-start = ((s32[128,1,4]{2,1,0:T(1,128)}), s32[128,1,4]{2,1,0:T(1,128)S(1)}, u32[]{:S(2)}, u32[]{:S(2)}) async-start(s32[128,1,4]{2,1,0:T(1,128)} %bitcast), calls=%async_computation | async-start | bytes 131072 | tf_op jit(solution)/shard_map/all_to_all | solution.py:30
  26.5 1.6 gather_fusion.1
  28.0 0.8 convert_element_type.143
  28.8 7.2 %all-to-all-done = s32[128,1,4]{2,1,0:T(1,128)S(1)} async-done(((s32[128,1,4]{2,1,0:T(1,128)}), s32[128,1,4]{2,1,0:T(1,128)S(1)}, u32[]{:S(2)}, u32[]{:S(2)}) %all-to-all-start) | async-done | bytes 2080 | tf_op jit(solution)/shard_map/all_to_all | solution.py:30
  36.0 4.6 all-to-all-start.1
  40.6 0.5 broadcast.68
  41.2 0.8 reduce.3
  42.1 9.5 %all-to-all-done.1 = bf16[128,4,256]{2,1,0:T(4,128)(2,1)S(1)} async-done(((bf16[128,4,256]{2,1,0:T(4,128)(2,1)}), bf16[128,4,256]{2,1,0:T(4,128)(2,1)S(1)}, u32[]{:S(2)}, u32[]{:S(2)}) %all-to-all-start.1) | async-done | bytes 262176 | tf_op jit(solution)/shard_map/all_to_all | solution.py:23
  51.6 2.4 scatter_custom_fusion
  54.0 0.2 fusion.33
  54.3 1.1 stack.16
  55.4 3.7 all-to-all-start.2
  59.2 11.5 %fusion.67 = (bf16[1,1,8,128,1,16,128]{6,5,4,3,2,1,0:T(8,128)(2,1)}, bf16[1,1,8,128,1,16,128]{6,5,4,3,2,1,0:T(8,128)(2,1)}, bf16[1,1,8,128,1,16,128]{6,5,4,3,2,1...) fusion(bf16[3,1,8,128,1,16,128]{6,5,4,3,2,1,0:T(8,128)(2,1)} %p, ...), kind=kLoop, calls=%fused_computation.98 | loop fusion | flops 6291456 | bytes 37749504 | tf_op jit(solution)/shard_map/slice | solution.py:47
  70.7 5.8 %all-to-all-done.2 = bf16[16,128,256]{2,1,0:T(8,128)(2,1)S(1)} async-done(((bf16[16,128,256]{2,1,0:T(8,128)(2,1)}), bf16[16,128,256]{2,1,0:T(8,128)(2,1)S(1)}, u32[]{:S(2)}, u32[]{:S(2)}) %all-to-all-start.2) | async-done | bytes 1048608 | tf_op jit(solution)/shard_map/all_to_all | solution.py:67
  76.5 4.3 fusion.24
  80.9 27.7 %reduce-scatter.13.cloned.1.call-done = bf16[128,256]{1,0:T(8,128)(2,1)} async-done(((bf16[1024,256]{1,0:T(8,128)(2,1)}), bf16[128,256]{1,0:T(8,128)(2,1)}) %reduce-scatter.13.cloned.1.call-update) | async-done | bytes 65552 | tf_op jit(solution)/shard_map/reduce_scatter | solution.py:77
  108.6 1.0 fusion.34
  109.8 20.9 %all_to_all.29 = bf16[16,128,256]{2,1,0:T(8,128)(2,1)S(1)} all-to-all(bf16[16,128,256]{2,1,0:T(8,128)(2,1)S(1)} %stack.17), channel_id=1, replica_groups=mesh['row'=16,'col'=8] {'row'}, dimensions={0} | all-to-all | bytes 2097152 | tf_op jit(solution)/shard_map/all_to_all | solution.py:67
  130.7 4.2 fusion.27
  135.0 29.7 %reduce-scatter.15.cloned.1.call-done = bf16[128,256]{1,0:T(8,128)(2,1)} async-done(((bf16[1024,256]{1,0:T(8,128)(2,1)}), bf16[128,256]{1,0:T(8,128)(2,1)}) %reduce-scatter.15.cloned.1.call-update) | async-done | bytes 65552 | tf_op jit(solution)/shard_map/reduce_scatter | solution.py:77
  164.7 1.0 fusion.35
  166.0 20.9 %all_to_all.30 = bf16[16,128,256]{2,1,0:T(8,128)(2,1)S(1)} all-to-all(bf16[16,128,256]{2,1,0:T(8,128)(2,1)S(1)} %stack.18), channel_id=1, replica_groups=mesh['row'=16,'col'=8] {'row'}, dimensions={0} | all-to-all | bytes 2097152 | tf_op jit(solution)/shard_map/all_to_all | solution.py:67
  186.8 4.2 fusion.30
  191.1 29.7 %reduce-scatter.17.cloned.1.call-done = bf16[128,256]{1,0:T(8,128)(2,1)} async-done(((bf16[1024,256]{1,0:T(8,128)(2,1)}), bf16[128,256]{1,0:T(8,128)(2,1)}) %reduce-scatter.17.cloned.1.call-update) | async-done | bytes 65552 | tf_op jit(solution)/shard_map/reduce_scatter | solution.py:77
  220.8 1.2 convolution_convert_fusion.3
  222.0 12.6 %all_gather.9 = bf16[1024,256]{0,1:T(8,128)(2,1)S(1)} all-gather(bf16[128,256]{0,1:T(8,128)(2,1)S(1)} %bitcast.142), channel_id=1, replica_groups=mesh['row'=16,'col'=8] {'col'}, dimensions={0}, use_global_device_ids=true | all-gather | bytes 589824 | tf_op jit(solution)/shard_map/all_gather | solution.py:91
  234.5 0.6 mul.74
  235.1 4.2 fusion.23
  239.4 73.7 %reduce-scatter.19.cloned.1.call-done = bf16[128,256]{1,0:T(8,128)(2,1)} async-done(((bf16[2048,256]{1,0:T(8,128)(2,1)}), bf16[128,256]{1,0:T(8,128)(2,1)}) %reduce-scatter.19.cloned.1.call-update) | async-done | bytes 65552
  313.0 0.9 copy.26
  314.0 0.1 convolution_convert_fusion.2
  314.2 13.5 %all_gather.10 = bf16[1024,256]{0,1:T(8,128)(2,1)S(1)} all-gather(bf16[128,256]{0,1:T(8,128)(2,1)S(1)} %bitcast.144), channel_id=1, replica_groups=mesh['row'=16,'col'=8] {'col'}, dimensions={0}, use_global_device_ids=true | all-gather | bytes 589824 | tf_op jit(solution)/shard_map/all_gather | solution.py:91
  327.7 0.6 mul.68
  328.3 4.1 fusion.22
  332.4 71.1 %reduce-scatter.21.cloned.1.call-done = bf16[128,256]{1,0:T(8,128)(2,1)} async-done(((bf16[2048,256]{1,0:T(8,128)(2,1)}), bf16[128,256]{1,0:T(8,128)(2,1)}) %reduce-scatter.21.cloned.1.call-update) | async-done | bytes 65552
  403.5 0.9 copy.28
  404.5 0.1 convolution_convert_fusion.1
  404.6 13.7 %all_gather.11 = bf16[1024,256]{0,1:T(8,128)(2,1)S(1)} all-gather(bf16[128,256]{0,1:T(8,128)(2,1)S(1)} %bitcast.146), channel_id=1, replica_groups=mesh['row'=16,'col'=8] {'col'}, dimensions={0}, use_global_device_ids=true | all-gather | bytes 589824 | tf_op jit(solution)/shard_map/all_gather | solution.py:91
  418.4 0.6 mul.62
  419.0 4.1 fusion.21
  423.1 71.1 %reduce-scatter.23.cloned.1.call-done = bf16[128,256]{1,0:T(8,128)(2,1)} async-done(((bf16[2048,256]{1,0:T(8,128)(2,1)}), bf16[128,256]{1,0:T(8,128)(2,1)}) %reduce-scatter.23.cloned.1.call-update) | async-done | bytes 65552
  494.2 0.9 copy.30
  495.1 0.1 fusion.36
  495.3 0.9 copy.24
  (40 shorter events, 1.1 us)
Async XLA Ops:
  6.5 19.9 %copy-start = (f32[512,256]{1,0:T(8,128)S(1)}, f32[512,256]{1,0:T(8,128)}, u32[]{:S(2)}) copy-start(f32[512,256]{1,0:T(8,128)} %param.5) | copy-start | bytes 1572868
  6.5 34.1 %copy-start.6 = (s32[3,1,8,1,16]{4,3,2,1,0:T(1,128)S(1)}, s32[3,1,8,1,16]{4,3,2,1,0:T(1,128)}, u32[]{:S(2)}) copy-start(s32[3,1,8,1,16]{4,3,2,1,0:T(1,128)} %param.9) | copy-start | bytes 4612
  6.5 47.4 %copy-start.5 = (bf16[4,1,128,128]{3,2,1,0:T(8,128)(2,1)S(1)}, bf16[4,1,128,128]{3,2,1,0:T(8,128)(2,1)}, u32[]{:S(2)}) copy-start(bf16[4,1,128,128]{3,2,1,0:T(8,128)(2,1)} %param.7) | copy-start | bytes 393220
  15.3 20.6 %all-to-all-start = ((s32[128,1,4]{2,1,0:T(1,128)}), s32[128,1,4]{2,1,0:T(1,128)S(1)}, u32[]{:S(2)}, u32[]{:S(2)}) async-start(s32[128,1,4]{2,1,0:T(1,128)} %bitcast), calls=%async_computation | async-start | bytes 131072 | tf_op jit(solution)/shard_map/all_to_all | solution.py:30
  36.0 15.6 %all-to-all-start.1 = ((bf16[128,4,256]{2,1,0:T(4,128)(2,1)}), bf16[128,4,256]{2,1,0:T(4,128)(2,1)S(1)}, u32[]{:S(2)}, u32[]{:S(2)}) async-start(bf16[128,4,256]{2,1,0:T(4,128)(2,1)} %convert_element_type.143), calls=%async_computation.1 | async-start | bytes 524288 | tf_op jit(solution)/shard_map/all_to_all | solution.py:23
  55.4 21.1 %all-to-all-start.2 = ((bf16[16,128,256]{2,1,0:T(8,128)(2,1)}), bf16[16,128,256]{2,1,0:T(8,128)(2,1)S(1)}, u32[]{:S(2)}, u32[]{:S(2)}) async-start(bf16[16,128,256]{2,1,0:T(8,128)(2,1)} %stack.16), calls=%async_computation.2 | async-start | bytes 2097152 | tf_op jit(solution)/shard_map/all_to_all | solution.py:67
  59.1 49.5 %reduce-scatter.13.cloned.1.call-start = ((), (), s32[]{:S(2)}) async-start(), calls=%async_computation.11 | async-start | bytes 589824 | tf_op jit(solution)/shard_map/reduce_scatter | solution.py:77
  80.8 83.9 %reduce-scatter.15.cloned.1.call-start = ((), (), s32[]{:S(2)}) async-start(), calls=%async_computation.12 | async-start | bytes 589824 | tf_op jit(solution)/shard_map/reduce_scatter | solution.py:77
  134.9 85.8 %reduce-scatter.17.cloned.1.call-start = ((), (), s32[]{:S(2)}) async-start(), calls=%async_computation.13 | async-start | bytes 589824 | tf_op jit(solution)/shard_map/reduce_scatter | solution.py:77
  191.1 122.0 %reduce-scatter.19.cloned.1.call-start = ((), (), s32[]{:S(2)}) async-start(), calls=%async_computation.14 | async-start | bytes 1114112
  222.0 13.2 %copy-start.4 = (bf16[1,1,8,128,1,16,128]{6,5,4,3,2,1,0:T(8,128)(2,1)S(1)}, bf16[1,1,8,128,1,16,128]{6,5,4,3,2,1,0:T(8,128)(2,1)}, u32[]{:S(2)}) copy-start(bf16[1,1,8,128,1,16,128]{6,5,4,3,2,1,0:T(8,128)(2,1)} %get-tuple-element.11) | copy-start | bytes 12582916
  239.3 164.2 %reduce-scatter.21.cloned.1.call-start = ((), (), s32[]{:S(2)}) async-start(), calls=%async_computation.15 | async-start | bytes 1114112
  314.0 14.3 %copy-start.3 = (bf16[1,1,8,128,1,16,128]{6,5,4,3,2,1,0:T(8,128)(2,1)S(1)}, bf16[1,1,8,128,1,16,128]{6,5,4,3,2,1,0:T(8,128)(2,1)}, u32[]{:S(2)}) copy-start(bf16[1,1,8,128,1,16,128]{6,5,4,3,2,1,0:T(8,128)(2,1)} %get-tuple-element.12) | copy-start | bytes 12582916
  332.4 161.8 %reduce-scatter.23.cloned.1.call-start = ((), (), s32[]{:S(2)}) async-start(), calls=%async_computation.16 | async-start | bytes 1114112
  404.5 14.5 %copy-start.2 = (bf16[1,1,8,128,1,16,128]{6,5,4,3,2,1,0:T(8,128)(2,1)S(1)}, bf16[1,1,8,128,1,16,128]{6,5,4,3,2,1,0:T(8,128)(2,1)}, u32[]{:S(2)}) copy-start(bf16[1,1,8,128,1,16,128]{6,5,4,3,2,1,0:T(8,128)(2,1)} %get-tuple-element.7) | copy-start | bytes 12582916
  419.0 77.2 %copy-start.1 = (f32[512,256]{1,0:T(8,128)S(1)}, f32[512,256]{1,0:T(8,128)}, u32[]{:S(2)}) copy-start(f32[512,256]{1,0:T(8,128)} %param.5) | copy-start | bytes 1572868
Sparse Core Ops, SparseCore 0:
  81.0 27.5 reduce-scatter.12
  135.1 29.5 reduce-scatter.14
  191.2 29.5 reduce-scatter.16
  239.4 73.5 reduce-scatter.18
  332.5 70.9 reduce-scatter.20
  423.2 70.9 reduce-scatter.22
